TPU v7x, 256 devices: a whole 4x4x8 slice. The times are simulated.
256 devices in a mesh: section: 2 (over core), req: 16 (over x, y), head: 8 (over z).
Axes of the slice: x: 4, y: 4, z: 8, core: 2. Of those that a mesh axis runs over, the one named last changes fastest.
Arguments:
- tokens: bfloat16 [256, 8192], P(None, 'req'), may hold values from -14 to 14
- attention_gain: bfloat16 [2, 8192], P('section', 'req'), may hold values from 0.099609375 to 1.8984375
- query_key_value_weight: bfloat16 [2, 8192, 8, 1280], P('section', 'req', 'head'), may hold values from -0.0625 to 0.0625
- head_output_weight: bfloat16 [2, 8, 1024, 8192], P('section', 'head', None, 'req'), may hold values from -0.0625 to 0.0625
- feedforward_gain: bfloat16 [2, 8192], P('section', 'req'), may hold values from 0.099609375 to 1.8984375
- gate_up: bfloat16 [2, 8192, 2, 14336], P('section', 'req', None, 'head'), may hold values from -0.0625 to 0.0625
- down_weight: bfloat16 [2, 14336, 8192], P('section', 'head', 'req'), may hold values from -0.046875 to 0.046875
- packed_cache: bfloat16 [2, 32768, 8, 256], P('section', 'req', 'head'), may hold values from -70 to 70
- long_cache: bfloat16 [2, 2, 32768, 8, 256], P('section', None, 'req', 'head'), may hold values from -70 to 70
- lengths: int32 [16, 16], P('req'), may hold values from 1 to 256, 2048 in all within a row
- long_split: int32 [2, 16], P(None, 'req'), may hold values from 1 to 2048, 16384 in all within a row
Outputs:
- layer_outputs: bfloat16 [2, 256, 8192], P('section', None, 'req')
Inputs may be any that keep to these rules, and one draw needn't show every extreme that they name: Row g holds the lengths of the 16 requests of request group g in order; they sum to 2048, and the requests' keys fill that group's 2048 slots of packed_cache one request after another. `long_split`: entry (j, g) counts the live slots, the first ones, of group g's 2048 slots of long request j; each row sums to 16384.
All inputs are finite; a program needn't handle non-finite values.
Results may differ from a plain program's by a relative error of at most 0.04.
Values may be sent and summed in bfloat16 or wider, within the bound.
A program may use at most 64 MiB of HBM per device.

v0:
```python
import math
import jax
import jax.numpy as jnp
from jax import lax
from jax.sharding import PartitionSpec as P

MODEL_WIDTH = 8192
QUERY_HEADS = 64
KEY_VALUE_HEADS = 8
HEAD_SIZE = 128
LONG = 16384
EPSILON = 1e-05


def merged(part, axis, combine):
    gathered = jax.tree.map(lambda a: lax.all_gather(a, axis), part)

    def take(source):
        return jax.tree.map(lambda a: lax.dynamic_index_in_dim(a, source, 0, False), gathered)

    return lax.fori_loop(
        1, lax.axis_size(axis), lambda source, state: combine(state, take(source)), take(0)
    )


def shifted(value, axis, by):
    peers = lax.axis_size(axis)
    pairs = [(i, i + by) for i in range(peers) if 0 <= i + by < peers]
    return lax.ppermute(value, axis, pairs)


def rotate(values, position):
    half_dim = values.shape[-1] // 2
    freq_ids = jnp.arange(half_dim).astype(jnp.float32)
    inverse = 1.0 / 10000.0 ** (freq_ids * 2.0 / values.shape[-1])
    angles = position.astype(jnp.float32)[:, None] * inverse[None, :]
    cosine = jnp.cos(angles)[:, None, None, :]
    sine_part = jnp.sin(angles)[:, None, None, :]
    lower_half = values[..., :half_dim]
    upper_half = values[..., half_dim:]
    return jnp.concatenate(
        [
            lower_half * cosine - upper_half * sine_part,
            upper_half * cosine + lower_half * sine_part,
        ],
        -1,
    )


def add_pair(earlier, second_part):
    return earlier + second_part


def combine_partial(earlier, second_part):
    peak = jnp.maximum(earlier[0], second_part[0])
    left_factor = jnp.exp(earlier[0] - peak)
    right_factor = jnp.exp(second_part[0] - peak)
    softmax_total = earlier[1] * left_factor + second_part[1] * right_factor
    weighted_sum = earlier[2] * left_factor[..., None] + second_part[2] * right_factor[..., None]
    return (peak, softmax_total, weighted_sum)


def over_requests(values, combiner):
    return merged(values, "req", combiner)


def rows_apply(values, row_fn):
    return row_fn(lax.all_gather(values, "req", axis=0, tiled=True), jnp.int32(0))


def rows_project(term_fn, row_count):
    return lax.psum_scatter(
        term_fn(jnp.int32(0), row_count * lax.axis_size("req")),
        "req",
        scatter_dimension=0,
        tiled=True,
    )


def head_total(values):
    return lax.psum(values, "head")


def keep_rows(piece_rows, start_row):
    return piece_rows


def norm_rows(values, gain_row):
    floats = values.astype(jnp.float32)
    squares = over_requests(jnp.sum(floats * floats, axis=-1), add_pair)
    return (
        floats * lax.rsqrt(squares / MODEL_WIDTH + EPSILON)[:, None] * gain_row.astype(jnp.float32)
    ).astype(jnp.bfloat16)


def decoder_layer(
    inputs,
    micro_batch,
    attention_gain,
    query_key_value_weight,
    head_output_weight,
    feedforward_gain,
    gate_up,
    down_weight,
    packed_cache,
    long_cache,
    lengths,
    long_split,
):
    req_count = lax.axis_size("req")
    group_index = lax.axis_index("req")
    blocks = inputs.shape[0] // req_count
    columns = query_key_value_weight.shape[1]
    kv_local = query_key_value_weight.shape[2]
    requests_per_group = QUERY_HEADS // KEY_VALUE_HEADS
    score_scale = 1.0 / math.sqrt(HEAD_SIZE)
    normalized_input = norm_rows(inputs, attention_gain[0])
    in_weights = query_key_value_weight[0].reshape(
        columns, kv_local * (requests_per_group + 2) * HEAD_SIZE
    )

    def qkv_term(start_row, row_count):
        return jnp.dot(normalized_input, in_weights, preferred_element_type=jnp.float32)

    projected_rows = rows_project(qkv_term, blocks).reshape(
        blocks, kv_local, requests_per_group + 2, HEAD_SIZE
    )
    local_rows = jnp.arange(blocks)
    row_lengths = lengths[0]
    owner_long = (group_index == 0) | (group_index == req_count // 2)
    long_row = (local_rows == 0) & (micro_batch == 0) & owner_long
    position = row_lengths + jnp.where(long_row, LONG, 0).astype(jnp.int32)
    queries = rotate(projected_rows[:, :, :requests_per_group], position).astype(jnp.bfloat16)
    new_key = rotate(projected_rows[:, :, requests_per_group : requests_per_group + 1], position)[
        :, :, 0
    ].astype(jnp.bfloat16)
    new_value = projected_rows[:, :, requests_per_group + 1].astype(jnp.bfloat16)
    gathered = rows_apply(
        queries[0:1].reshape(1, kv_local * requests_per_group * HEAD_SIZE), keep_rows
    )
    long_queries = jnp.stack([gathered[0], gathered[req_count // 2]]).reshape(
        2, kv_local, requests_per_group, HEAD_SIZE
    )
    far_cache = long_cache[0]
    far_live = (jnp.arange(far_cache.shape[1])[None, :] < long_split[:, 0][:, None])[
        :, None, None, :
    ]
    far_scores = (
        jnp.einsum(
            "jkhd,jpkd->jkhp",
            long_queries,
            far_cache[..., :HEAD_SIZE],
            preferred_element_type=jnp.float32,
        )
        * score_scale
    )
    far_max = jnp.max(jnp.where(far_live, far_scores, -jnp.inf), axis=-1)
    far_weights = jnp.where(
        far_live, jnp.exp(jnp.where(far_live, far_scores - far_max[..., None], 0.0)), 0.0
    ).astype(jnp.bfloat16)
    far_totals = jnp.sum(far_weights.astype(jnp.float32), axis=-1)
    far_summed = jnp.einsum(
        "jkhp,jpkd->jkhd",
        far_weights,
        far_cache[..., HEAD_SIZE:],
        preferred_element_type=jnp.float32,
    )
    far_max, far_totals, far_summed = over_requests(
        (far_max, far_totals, far_summed), combine_partial
    )
    far_index = jnp.where(group_index == 0, 0, 1)
    chosen_max = lax.dynamic_index_in_dim(far_max, far_index, 0, keepdims=False)
    chosen_totals = lax.dynamic_index_in_dim(far_totals, far_index, 0, keepdims=False)
    chosen_summed = lax.dynamic_index_in_dim(far_summed, far_index, 0, keepdims=False)
    pack_part = packed_cache[0]
    seg_ends = jnp.cumsum(lengths[0])
    slot_ids = jnp.arange(pack_part.shape[0])
    slot_owner = jnp.sum((slot_ids[:, None] >= seg_ends[None, :]).astype(jnp.int32), axis=1)
    request_ids = micro_batch * blocks + local_rows
    in_segment = (slot_owner[None, :] == request_ids[:, None])[:, None, None, :]
    scores = (
        jnp.einsum(
            "rkhd,pkd->rkhp",
            queries,
            pack_part[..., :HEAD_SIZE],
            preferred_element_type=jnp.float32,
        )
        * score_scale
    )
    own_score = (
        jnp.einsum("rkhd,rkd->rkh", queries, new_key, preferred_element_type=jnp.float32)
        * score_scale
    )
    row_max = jnp.maximum(jnp.max(jnp.where(in_segment, scores, -jnp.inf), axis=-1), own_score)
    long_mask = long_row[:, None, None]
    row_max = jnp.where(long_mask, jnp.maximum(row_max, chosen_max[None]), row_max)
    weights = jnp.where(
        in_segment, jnp.exp(jnp.where(in_segment, scores - row_max[..., None], 0.0)), 0.0
    ).astype(jnp.bfloat16)
    own_weights = jnp.exp(own_score - row_max).astype(jnp.bfloat16)
    far_factor = jnp.where(
        long_mask, jnp.exp(jnp.where(long_mask, chosen_max[None] - row_max, 0.0)), 0.0
    )
    softmax_total = (
        jnp.sum(weights.astype(jnp.float32), axis=-1)
        + own_weights.astype(jnp.float32)
        + far_factor * chosen_totals[None]
    )
    weighted_sum = jnp.einsum(
        "rkhp,pkd->rkhd", weights, pack_part[..., HEAD_SIZE:], preferred_element_type=jnp.float32
    )
    weighted_sum = (
        weighted_sum
        + own_weights.astype(jnp.float32)[..., None] * new_value.astype(jnp.float32)[:, :, None, :]
    )
    weighted_sum = weighted_sum + far_factor[..., None] * chosen_summed[None]
    attended_heads = (
        (weighted_sum / softmax_total[..., None])
        .astype(jnp.bfloat16)
        .reshape(blocks, kv_local * requests_per_group * HEAD_SIZE)
    )
    out_weights = head_output_weight[0].reshape(kv_local * requests_per_group * HEAD_SIZE, columns)

    def project_heads(piece_rows, start_row):
        return jnp.dot(piece_rows, out_weights, preferred_element_type=jnp.float32)

    attended = head_total(rows_apply(attended_heads, project_heads))
    residual = (inputs.astype(jnp.float32) + attended).astype(jnp.bfloat16)
    normed_two = norm_rows(residual, feedforward_gain[0])
    ff_weights = gate_up[0].reshape(columns, -1)

    def ff_term(start_row, row_count):
        return jnp.dot(normed_two, ff_weights, preferred_element_type=jnp.float32)

    gate_and_up = rows_project(ff_term, blocks)
    hidden_width = gate_and_up.shape[1] // 2
    hidden = (jax.nn.silu(gate_and_up[:, :hidden_width]) * gate_and_up[:, hidden_width:]).astype(
        jnp.bfloat16
    )
    lower_weights = down_weight[0]

    def project_hidden(piece_rows, start_row):
        return jnp.dot(piece_rows, lower_weights, preferred_element_type=jnp.float32)

    lowered = head_total(rows_apply(hidden, project_hidden))
    return (residual.astype(jnp.float32) + lowered).astype(jnp.bfloat16)


def local(
    tokens,
    attention_gain,
    query_key_value_weight,
    head_output_weight,
    feedforward_gain,
    gate_up,
    down_weight,
    packed_cache,
    long_cache,
    lengths,
    long_split,
):
    req_count = lax.axis_size("req")
    section_index = lax.axis_index("section")
    batch_count = 1
    per_group = tokens.shape[0] // req_count
    blocks = per_group // batch_count
    columns = tokens.shape[1]
    token_grid = tokens.reshape(req_count, per_group, columns)
    result = jnp.zeros_like(token_grid)
    incoming = jnp.zeros((req_count * blocks, columns), jnp.bfloat16)
    for phase_step in range(batch_count + 1):
        micro_batch = phase_step - section_index
        is_active = (micro_batch >= 0) & (micro_batch < batch_count)
        micro_batch = jnp.clip(micro_batch, 0, batch_count - 1)
        new_batch = token_grid.reshape(req_count * blocks, columns)
        inputs = jnp.where(section_index == 0, new_batch, incoming)
        output = decoder_layer(
            inputs,
            micro_batch,
            attention_gain,
            query_key_value_weight,
            head_output_weight,
            feedforward_gain,
            gate_up,
            down_weight,
            packed_cache,
            long_cache,
            lengths,
            long_split,
        )
        placed = output.reshape(req_count, blocks, columns)
        result = jnp.where(is_active, placed, result)
        if phase_step < batch_count:
            incoming = shifted(output, "section", 1)
    return result.reshape(1, req_count * per_group, columns)


def solution(mesh):
    placed = (
        P(None, "req"),
        P("section", "req"),
        P("section", "req", "head", None),
        P("section", "head", None, "req"),
        P("section", "req"),
        P("section", "req", None, "head"),
        P("section", "head", "req"),
        P("section", "req", "head", None),
        P("section", None, "req", "head", None),
        P("req", None),
        P(None, "req"),
    )
    return jax.shard_map(
        local, mesh=mesh, in_specs=placed, out_specs=P("section", None, "req"), check_vma=False
    )
```

profile of v0, /device:TPU:2, one launch (start us, length us, event | category | flops | bytes accessed | tf_op | source)
XLA Modules:
  0.0 1032.9 jit_solution(9253363095233518662)
XLA Ops:
  6.5 1.2 fusion.34
  7.8 23.3 %all-gather.10 = f32[16,1,256]{2,1,0:T(1,128)S(1)} all-gather(f32[1,1,256]{2,1,0:T(1,128)S(1)} %bitcast.379), channel_id=2, replica_groups=mesh['section'=2,'req'=16,'head'=8] {'req'}, dimensions={0}, use_global_device_ids=true | all-gather | bytes 17408 | tf_op jit(solution)/shard_map/all_gather | solution.py:16
  32.5 3.0 fusion.18
  36.4 78.1 %reduce-scatter.5.cloned.1.call-done = f32[16,1280]{1,0:T(8,128)} async-done(((f32[256,1280]{1,0:T(8,128)}), f32[16,1280]{1,0:T(8,128)}) %reduce-scatter.5.cloned.1.call-update) | async-done | bytes 81936 | tf_op jit(solution)/shard_map/reduce_scatter | solution.py:72
  115.7 21.4 %all-gather.11 = bf16[16,1,1024]{2,1,0:T(2,128)(2,1)S(1)} all-gather(bf16[1,1,1024]{2,1,0:T(2,128)(2,1)S(1)} %reshape.774), channel_id=1, replica_groups=mesh['section'=2,'req'=16,'head'=8] {'req'}, dimensions={0}, use_global_device_ids=true | all-gather | bytes 34816 | tf_op jit(solution)/shard_map/all_gather | solution.py:68
  137.2 1.7 select_reduce_fusion.3
  139.1 1.5 fusion.33
  140.6 22.6 %all-gather.12 = f32[16,2,8]{2,1,0:T(2,128)S(1)} all-gather(f32[1,2,8]{2,1,0:T(2,128)S(1)} %bitcast.371), channel_id=3, replica_groups=mesh['section'=2,'req'=16,'head'=8] {'req'}, dimensions={0}, use_global_device_ids=true | all-gather | bytes 1088 | tf_op jit(solution)/shard_map/all_gather | solution.py:16
  163.2 21.1 %all-gather.13 = f32[16,2,8]{2,1,0:T(2,128)S(1)} all-gather(f32[1,2,8]{2,1,0:T(2,128)S(1)} %bitcast.375), channel_id=4, replica_groups=mesh['section'=2,'req'=16,'head'=8] {'req'}, dimensions={0}, use_global_device_ids=true | all-gather | bytes 1088 | tf_op jit(solution)/shard_map/all_gather | solution.py:16
  184.3 23.0 %all-gather.3 = f32[32,8,128]{2,1,0:T(8,128)S(1)} all-gather(f32[2,8,128]{2,1,0:T(8,128)S(1)} %fusion.33), channel_id=5, replica_groups=mesh['section'=2,'req'=16,'head'=8] {'req'}, dimensions={0}, use_global_device_ids=true | all-gather | bytes 139264 | tf_op jit(solution)/shard_map/all_gather | solution.py:16
  207.4 1.7 while.99
  211.0 21.7 %all_gather.87 = bf16[256,1024]{1,0:T(8,128)(2,1)S(1)} all-gather(bf16[16,1024]{1,0:T(8,128)(2,1)S(1)} %bitcast.340), channel_id=1, replica_groups=mesh['section'=2,'req'=16,'head'=8] {'req'}, dimensions={0}, use_global_device_ids=true | all-gather | bytes 557056 | tf_op jit(solution)/shard_map/all_gather | solution.py:68
  232.7 1.3 fusion.30
  234.1 4.5 copy.75
  238.6 69.5 %all-reduce.5.cloned.1.call-done = f32[256,512]{1,0:T(8,128)} async-done(((f32[256,512]{1,0:T(8,128)}), f32[256,512]{1,0:T(8,128)}) %all-reduce.5.cloned.1.call-update) | async-done | bytes 524304 | tf_op jit(solution)/shard_map/psum | solution.py:81
  308.0 1.2 fusion.38
  309.3 23.0 %all-gather.14 = f32[16,1,256]{2,1,0:T(1,128)S(1)} all-gather(f32[1,1,256]{2,1,0:T(1,128)S(1)} %bitcast.378), channel_id=6, replica_groups=mesh['section'=2,'req'=16,'head'=8] {'req'}, dimensions={0}, use_global_device_ids=true | all-gather | bytes 17408 | tf_op jit(solution)/shard_map/all_gather | solution.py:16
  333.0 5.0 fusion.57
  338.1 77.9 %reduce-scatter.7.cloned.1.call-done = f32[16,3584]{1,0:T(8,128)} async-done(((f32[256,3584]{1,0:T(8,128)}), f32[16,3584]{1,0:T(8,128)}) %reduce-scatter.7.cloned.1.call-update) | async-done | bytes 229392 | tf_op jit(solution)/shard_map/reduce_scatter | solution.py:72
  416.0 1.0 fusion.70
  417.0 23.0 %all_gather.90 = bf16[256,1792]{1,0:T(8,128)(2,1)S(1)} all-gather(bf16[16,1792]{1,0:T(8,128)(2,1)S(1)} %fusion.70), channel_id=1, replica_groups=mesh['section'=2,'req'=16,'head'=8] {'req'}, dimensions={0}, use_global_device_ids=true | all-gather | bytes 974848 | tf_op jit(solution)/shard_map/all_gather | solution.py:68
  440.1 1.4 fusion.14
  441.6 73.4 %all-reduce.7.cloned.1.call-done = f32[256,512]{1,0:T(8,128)} async-done(((f32[256,512]{1,0:T(8,128)}), f32[256,512]{1,0:T(8,128)}) %all-reduce.7.cloned.1.call-update) | async-done | bytes 524304 | tf_op jit(solution)/shard_map/psum | solution.py:81
  515.0 1.9 fusion.41
  516.9 2.0 collective-permute-start
  520.5 23.0 %all-gather.15 = f32[16,1,256]{2,1,0:T(1,128)S(1)} all-gather(f32[1,1,256]{2,1,0:T(1,128)S(1)} %bitcast.376), channel_id=7, replica_groups=mesh['section'=2,'req'=16,'head'=8] {'req'}, dimensions={0}, use_global_device_ids=true | all-gather | bytes 17408 | tf_op jit(solution)/shard_map/all_gather | solution.py:16
  544.2 2.6 fusion.16
  546.8 74.6 %reduce-scatter.9.cloned.1.call-done = f32[16,1280]{1,0:T(8,128)} async-done(((f32[256,1280]{1,0:T(8,128)}), f32[16,1280]{1,0:T(8,128)}) %reduce-scatter.9.cloned.1.call-update) | async-done | bytes 81936 | tf_op jit(solution)/shard_map/reduce_scatter | solution.py:72
  622.6 21.5 %all-gather.16 = bf16[16,1,1024]{2,1,0:T(2,128)(2,1)S(1)} all-gather(bf16[1,1,1024]{2,1,0:T(2,128)(2,1)S(1)} %reshape.784), channel_id=1, replica_groups=mesh['section'=2,'req'=16,'head'=8] {'req'}, dimensions={0}, use_global_device_ids=true | all-gather | bytes 34816 | tf_op jit(solution)/shard_map/all_gather | solution.py:68
  644.1 1.7 select_reduce_fusion.2
  646.0 1.5 fusion.32
  647.7 1.5 select_reduce_fusion
  649.5 22.6 %all-gather.17 = f32[16,2,8]{2,1,0:T(2,128)S(1)} all-gather(f32[1,2,8]{2,1,0:T(2,128)S(1)} %bitcast.370), channel_id=8, replica_groups=mesh['section'=2,'req'=16,'head'=8] {'req'}, dimensions={0}, use_global_device_ids=true | all-gather | bytes 1088 | tf_op jit(solution)/shard_map/all_gather | solution.py:16
  672.1 21.1 %all-gather.18 = f32[16,2,8]{2,1,0:T(2,128)S(1)} all-gather(f32[1,2,8]{2,1,0:T(2,128)S(1)} %bitcast.374), channel_id=9, replica_groups=mesh['section'=2,'req'=16,'head'=8] {'req'}, dimensions={0}, use_global_device_ids=true | all-gather | bytes 1088 | tf_op jit(solution)/shard_map/all_gather | solution.py:16
  693.2 22.9 %all-gather.8 = f32[32,8,128]{2,1,0:T(8,128)S(1)} all-gather(f32[2,8,128]{2,1,0:T(8,128)S(1)} %fusion.32), channel_id=10, replica_groups=mesh['section'=2,'req'=16,'head'=8] {'req'}, dimensions={0}, use_global_device_ids=true | all-gather | bytes 139264 | tf_op jit(solution)/shard_map/all_gather | solution.py:16
  716.1 1.7 while.102
  718.4 1.5 fusion.26
  719.9 22.1 %all_gather.100 = bf16[256,1024]{1,0:T(8,128)(2,1)S(1)} all-gather(bf16[16,1024]{1,0:T(8,128)(2,1)S(1)} %bitcast.341), channel_id=1, replica_groups=mesh['section'=2,'req'=16,'head'=8] {'req'}, dimensions={0}, use_global_device_ids=true | all-gather | bytes 557056 | tf_op jit(solution)/shard_map/all_gather | solution.py:68
  742.0 1.2 fusion.28
  743.4 73.8 %all-reduce.9.cloned.1.call-done = f32[256,512]{1,0:T(8,128)} async-done(((f32[256,512]{1,0:T(8,128)}), f32[256,512]{1,0:T(8,128)}) %all-reduce.9.cloned.1.call-update) | async-done | bytes 524304 | tf_op jit(solution)/shard_map/psum | solution.py:81
  817.2 1.2 fusion.46
  818.4 23.0 %all-gather.19 = f32[16,1,256]{2,1,0:T(1,128)S(1)} all-gather(f32[1,1,256]{2,1,0:T(1,128)S(1)} %bitcast.377), channel_id=11, replica_groups=mesh['section'=2,'req'=16,'head'=8] {'req'}, dimensions={0}, use_global_device_ids=true | all-gather | bytes 17408 | tf_op jit(solution)/shard_map/all_gather | solution.py:16
  842.1 5.0 fusion.54
  847.2 78.0 %reduce-scatter.11.cloned.1.call-done = f32[16,3584]{1,0:T(8,128)} async-done(((f32[256,3584]{1,0:T(8,128)}), f32[16,3584]{1,0:T(8,128)}) %reduce-scatter.11.cloned.1.call-update) | async-done | bytes 229392 | tf_op jit(solution)/shard_map/reduce_scatter | solution.py:72
  926.2 23.0 %all_gather.103 = bf16[256,1792]{1,0:T(8,128)(2,1)S(1)} all-gather(bf16[16,1792]{1,0:T(8,128)(2,1)S(1)} %fusion.69), channel_id=1, replica_groups=mesh['section'=2,'req'=16,'head'=8] {'req'}, dimensions={0}, use_global_device_ids=true | all-gather | bytes 974848 | tf_op jit(solution)/shard_map/all_gather | solution.py:68
  949.2 1.5 fusion.12
  950.7 73.4 %all-reduce.11.cloned.1.call-done = f32[256,512]{1,0:T(8,128)} async-done(((f32[256,512]{1,0:T(8,128)}), f32[256,512]{1,0:T(8,128)}) %all-reduce.11.cloned.1.call-update) | async-done | bytes 524304 | tf_op jit(solution)/shard_map/psum | solution.py:81
  1024.1 1.9 fusion.53
  (354 shorter events, 17.5 us)
Async XLA Ops:
  6.5 433.5 %copy-start = (bf16[1,1792,512]{2,1,0:T(8,128)(2,1)S(1)}, bf16[1,1792,512]{2,1,0:T(8,128)(2,1)}, u32[]{:S(2)}) copy-start(bf16[1,1792,512]{2,1,0:T(8,128)(2,1)} %param.29) | copy-start | bytes 5505028
  6.5 108.0 %reduce-scatter.5.cloned.1.call-start = ((), (), s32[]{:S(2)}) async-start(), calls=%async_computation.4 | async-start | bytes 1392640 | tf_op jit(solution)/shard_map/reduce_scatter | solution.py:72
  32.5 3.2 copy-start.9
  32.5 3.7 copy-start.10
  35.6 272.5 %all-reduce.5.cloned.1.call-start = ((), (), s32[]{:S(2)}) async-start(), calls=%async_computation.5 | async-start | bytes 1048576 | tf_op jit(solution)/shard_map/psum | solution.py:81
  35.9 173.5 %copy-start.7 = (bf16[1,2048,1,256]{3,1,2,0:T(8,128)(2,1)S(1)}, bf16[1,2048,1,256]{3,1,2,0:T(8,128)(2,1)}, u32[]{:S(2)}) copy-start(bf16[1,2048,1,256]{3,1,2,0:T(8,128)(2,1)} %param.30) | copy-start | bytes 3145732
  210.1 22.7 %copy-start.3 = (bf16[1,1,1024,512]{3,2,1,0:T(8,128)(2,1)S(1)}, bf16[1,1,1024,512]{3,2,1,0:T(8,128)(2,1)}, u32[]{:S(2)}) copy-start(bf16[1,1,1024,512]{3,2,1,0:T(8,128)(2,1)} %param.26) | copy-start | bytes 3145732
  234.0 182.0 %reduce-scatter.7.cloned.1.call-start = ((), (), s32[]{:S(2)}) async-start(), calls=%async_computation.6 | async-start | bytes 3899392 | tf_op jit(solution)/shard_map/reduce_scatter | solution.py:72
  234.1 4.5 copy-start.8
  234.1 74.0 %copy-start.2 = (bf16[256,512]{1,0:T(8,128)(2,1)S(1)}, bf16[256,512]{1,0:T(8,128)(2,1)}, u32[]{:S(2)}) copy-start(bf16[256,512]{1,0:T(8,128)(2,1)} %param.23) | copy-start | bytes 786436
  309.3 28.8 %copy-start.5 = (bf16[256,512]{1,0:T(8,128)(2,1)}, bf16[256,512]{1,0:T(8,128)(2,1)S(1)}, u32[]{:S(2)}) copy-start(bf16[256,512]{1,0:T(8,128)(2,1)S(1)} %get-tuple-element.859) | copy-start | bytes 786436
  338.1 176.9 %all-reduce.7.cloned.1.call-start = ((), (), s32[]{:S(2)}) async-start(), calls=%async_computation.7 | async-start | bytes 1048576 | tf_op jit(solution)/shard_map/psum | solution.py:81
  441.5 102.7 %copy-start.1 = (bf16[1,512,1,1280]{3,1,2,0:T(8,128)(2,1)S(1)}, bf16[1,512,1,1280]{3,1,2,0:T(8,128)(2,1)}, u32[]{:S(2)}) copy-start(bf16[1,512,1,1280]{3,1,2,0:T(8,128)(2,1)} %param.25) | copy-start | bytes 3932164
  441.5 179.9 %reduce-scatter.9.cloned.1.call-start = ((), (), s32[]{:S(2)}) async-start(), calls=%async_computation.8 | async-start | bytes 1392640 | tf_op jit(solution)/shard_map/reduce_scatter | solution.py:72
  516.9 2.8 collective-permute-start
  546.8 270.4 %all-reduce.9.cloned.1.call-start = ((), (), s32[]{:S(2)}) async-start(), calls=%async_computation.9 | async-start | bytes 1048576 | tf_op jit(solution)/shard_map/psum | solution.py:81
  717.9 24.1 %copy-start.4 = (bf16[1,1,1024,512]{3,2,1,0:T(8,128)(2,1)S(1)}, bf16[1,1,1024,512]{3,2,1,0:T(8,128)(2,1)}, u32[]{:S(2)}) copy-start(bf16[1,1,1024,512]{3,2,1,0:T(8,128)(2,1)} %param.26) | copy-start | bytes 3145732
  719.9 97.2 %copy-start.6 = (bf16[256,512]{1,0:T(8,128)(2,1)S(1)}, bf16[256,512]{1,0:T(8,128)(2,1)}, u32[]{:S(2)}) copy-start(bf16[256,512]{1,0:T(8,128)(2,1)} %get-tuple-element.857) | copy-start | bytes 786436
  743.3 181.8 %reduce-scatter.11.cloned.1.call-start = ((), (), s32[]{:S(2)}) async-start(), calls=%async_computation.10 | async-start | bytes 3899392 | tf_op jit(solution)/shard_map/reduce_scatter | solution.py:72
  847.2 176.9 %all-reduce.11.cloned.1.call-start = ((), (), s32[]{:S(2)}) async-start(), calls=%async_computation.11 | async-start | bytes 1048576 | tf_op jit(solution)/shard_map/psum | solution.py:81
Sparse Core Ops, SparseCore 0:
  35.7 78.7 reduce-scatter.4
  234.1 73.8 all-reduce.4
  338.2 77.7 reduce-scatter.6
  441.6 73.2 all-reduce.6
  546.9 74.4 reduce-scatter.8
  743.4 73.6 all-reduce.8
  847.3 77.8 reduce-scatter.10
  950.8 73.2 all-reduce.10
where the time goes:
time: 1030 us
  waiting for transfers between devices  600 us (58%)
  blocking collectives  358 us (35%)
  matrix products  31.8 us (3%)
  other arithmetic  17.6 us (2%)
  between operations  13.9 us (1%)
    reduce_scatter x4, waiting for transfers between devices, rows_project(): lax.psum_scatter(term_fn(jnp.int32(0), row_count * lax.axis_size('req')),...  309 us
    psum x4, waiting for transfers between devices, head_total(): return lax.psum(values, 'head')  290 us
    all_gather x10, blocking collectives, merged(): gathered = jax.tree.map(lambda a: lax.all_gather(a, axis), part)  226 us
    all_gather x6, blocking collectives, rows_apply(): lax.all_gather(values, 'req', axis=0, tiled=True)  133 us
  transfers between devices with their start and end apart: 9, of which 9 were waited for; matrix products, arithmetic and copies ran while one was open for 1% of the time, Pallas kernels for 0%

commit v1 on v0

--- a/solution.py
+++ b/solution.py
@@ -65,7 +65,12 @@
 
 
 def rows_apply(values, row_fn):
-    return row_fn(lax.all_gather(values, "req", axis=0, tiled=True), jnp.int32(0))
+    return row_fn(
+        jnp.concatenate(
+            lax.all_to_all(jnp.stack([values] * lax.axis_size("req")), "req", 0, 0), axis=0
+        ),
+        jnp.int32(0),
+    )
 
 
 def rows_project(term_fn, row_count):

time: 1030 us -> 987 us (0.958)
  blocking collectives: 358 us -> 288 us
  starting transfers between devices: 2.28 us -> 13.7 us
    all_gather x6 -> x0, blocking collectives: 133 us -> none  [rows_apply(): lax.all_gather(values, 'req', axis=0, tiled=True)]
    all_to_all x0 -> x4, blocking collectives: none -> 61.2 us  [rows_apply(): lax.all_to_all(jnp.stack([values] * lax.axis_size('req')), 'req', 0, 0)]
    all_to_all x0 -> x2, starting transfers between devices: none -> 11.4 us  [rows_apply(): lax.all_to_all(jnp.stack([values] * lax.axis_size('req')), 'req', 0, 0)]
  transfers between devices with their start and end apart: 9 -> 11, of which waited for: 9 -> 11; matrix products, arithmetic and copies ran while one was open for 1% -> 1% of each run, Pallas kernels for 0% -> 0%
where the time goes in v1:
time: 987 us; the launch traced here: 986 us
  waiting for transfers between devices  606 us (61%)
  blocking collectives  288 us (29%)
  matrix products  34.1 us (3%)
  other arithmetic  19.3 us (2%)
  between operations  13.9 us (1%)
  starting transfers between devices  13.7 us (1%)
    reduce_scatter x4, waiting for transfers between devices, rows_project(): lax.psum_scatter(term_fn(jnp.int32(0), row_count * lax.axis_size('req')),...  308 us
    psum x4, waiting for transfers between devices, head_total(): return lax.psum(values, 'head')  288 us
    all_gather x10, blocking collectives, merged(): gathered = jax.tree.map(lambda a: lax.all_gather(a, axis), part)  226 us
    all_to_all x4, blocking collectives, rows_apply(): lax.all_to_all(jnp.stack([values] * lax.axis_size('req')), 'req', 0, 0)  61.2 us
  transfers between devices with their start and end apart: 11, of which 11 were waited for; matrix products, arithmetic and copies ran while one was open for 1% of the time, Pallas kernels for 0%

profile of v1, /device:TPU:2, one launch (start us, length us, event | category | flops | bytes accessed | tf_op | source)
XLA Modules:
  0.0 986.1 jit_solution(3263592667374714678)
XLA Ops:
  7.8 23.3 %all-gather.10 = f32[16,1,256]{2,1,0:T(1,128)S(1)} all-gather(f32[1,1,256]{2,1,0:T(1,128)S(1)} %bitcast.379), channel_id=2, replica_groups=mesh['section'=2,'req'=16,'head'=8] {'req'}, dimensions={0}, use_global_device_ids=true | all-gather | bytes 17408 | tf_op jit(solution)/shard_map/all_gather | solution.py:16
  32.5 3.0 fusion.18
  36.4 78.2 %reduce-scatter.5.cloned.1.call-done = f32[16,1280]{1,0:T(8,128)} async-done(((f32[256,1280]{1,0:T(8,128)}), f32[16,1280]{1,0:T(8,128)}) %reduce-scatter.5.cloned.1.call-update) | async-done | bytes 81936 | tf_op jit(solution)/shard_map/reduce_scatter | solution.py:77
  117.9 5.7 all-to-all-start
  124.0 1.5 select_reduce_fusion.1
  125.5 4.3 all-to-all-done
  129.9 1.7 select_reduce_fusion.3
  131.8 1.5 fusion.33
  133.3 21.7 %all-gather.11 = f32[16,2,8]{2,1,0:T(2,128)S(1)} all-gather(f32[1,2,8]{2,1,0:T(2,128)S(1)} %bitcast.367), channel_id=3, replica_groups=mesh['section'=2,'req'=16,'head'=8] {'req'}, dimensions={0}, use_global_device_ids=true | all-gather | bytes 1088 | tf_op jit(solution)/shard_map/all_gather | solution.py:16
  155.0 21.4 %all-gather.12 = f32[16,2,8]{2,1,0:T(2,128)S(1)} all-gather(f32[1,2,8]{2,1,0:T(2,128)S(1)} %bitcast.375), channel_id=4, replica_groups=mesh['section'=2,'req'=16,'head'=8] {'req'}, dimensions={0}, use_global_device_ids=true | all-gather | bytes 1088 | tf_op jit(solution)/shard_map/all_gather | solution.py:16
  176.4 23.8 %all-gather.3 = f32[32,8,128]{2,1,0:T(8,128)S(1)} all-gather(f32[2,8,128]{2,1,0:T(8,128)S(1)} %fusion.33), channel_id=5, replica_groups=mesh['section'=2,'req'=16,'head'=8] {'req'}, dimensions={0}, use_global_device_ids=true | all-gather | bytes 139264 | tf_op jit(solution)/shard_map/all_gather | solution.py:16
  200.3 1.7 while.99
  202.6 1.6 fusion.27
  204.2 13.1 %all_to_all.30 = bf16[16,16,1024]{2,1,0:T(8,128)(2,1)S(1)} all-to-all(bf16[16,16,1024]{2,1,0:T(8,128)(2,1)S(1)} %stack.28), channel_id=1, replica_groups=mesh['section'=2,'req'=16,'head'=8] {'req'}, dimensions={0} | all-to-all | bytes 1048576 | tf_op jit(solution)/shard_map/all_to_all | solution.py:70
  217.3 1.2 fusion.30
  218.7 4.5 copy.74
  223.2 68.7 %all-reduce.5.cloned.1.call-done = f32[256,512]{1,0:T(8,128)} async-done(((f32[256,512]{1,0:T(8,128)}), f32[256,512]{1,0:T(8,128)}) %all-reduce.5.cloned.1.call-update) | async-done | bytes 524304 | tf_op jit(solution)/shard_map/psum | solution.py:86
  293.1 23.0 %all-gather.13 = f32[16,1,256]{2,1,0:T(1,128)S(1)} all-gather(f32[1,1,256]{2,1,0:T(1,128)S(1)} %bitcast.378), channel_id=6, replica_groups=mesh['section'=2,'req'=16,'head'=8] {'req'}, dimensions={0}, use_global_device_ids=true | all-gather | bytes 17408 | tf_op jit(solution)/shard_map/all_gather | solution.py:16
  316.8 5.0 fusion.57
  321.9 77.9 %reduce-scatter.7.cloned.1.call-done = f32[16,3584]{1,0:T(8,128)} async-done(((f32[256,3584]{1,0:T(8,128)}), f32[16,3584]{1,0:T(8,128)}) %reduce-scatter.7.cloned.1.call-update) | async-done | bytes 229392 | tf_op jit(solution)/shard_map/reduce_scatter | solution.py:77
  400.9 17.5 %all_to_all.31 = bf16[16,16,1792]{2,1,0:T(8,128)(2,1)S(1)} all-to-all(bf16[16,16,1792]{2,1,0:T(8,128)(2,1)S(1)} %stack.29), channel_id=1, replica_groups=mesh['section'=2,'req'=16,'head'=8] {'req'}, dimensions={0} | all-to-all | bytes 1835008 | tf_op jit(solution)/shard_map/all_to_all | solution.py:70
  418.4 1.4 fusion.14
  419.9 73.1 %all-reduce.7.cloned.1.call-done = f32[256,512]{1,0:T(8,128)} async-done(((f32[256,512]{1,0:T(8,128)}), f32[256,512]{1,0:T(8,128)}) %all-reduce.7.cloned.1.call-update) | async-done | bytes 524304 | tf_op jit(solution)/shard_map/psum | solution.py:86
  493.0 1.9 fusion.41
  494.9 2.0 collective-permute-start
  498.5 23.0 %all-gather.14 = f32[16,1,256]{2,1,0:T(1,128)S(1)} all-gather(f32[1,1,256]{2,1,0:T(1,128)S(1)} %bitcast.376), channel_id=7, replica_groups=mesh['section'=2,'req'=16,'head'=8] {'req'}, dimensions={0}, use_global_device_ids=true | all-gather | bytes 17408 | tf_op jit(solution)/shard_map/all_gather | solution.py:16
  522.2 2.6 fusion.16
  524.8 74.7 %reduce-scatter.9.cloned.1.call-done = f32[16,1280]{1,0:T(8,128)} async-done(((f32[256,1280]{1,0:T(8,128)}), f32[16,1280]{1,0:T(8,128)}) %reduce-scatter.9.cloned.1.call-update) | async-done | bytes 81936 | tf_op jit(solution)/shard_map/reduce_scatter | solution.py:77
  602.2 5.7 all-to-all-start.3
  608.3 1.5 select_reduce_fusion
  609.9 4.3 all-to-all-done.3
  614.2 1.7 select_reduce_fusion.2
  616.1 1.5 fusion.32
  617.6 21.7 %all-gather.15 = f32[16,2,8]{2,1,0:T(2,128)S(1)} all-gather(f32[1,2,8]{2,1,0:T(2,128)S(1)} %bitcast.366), channel_id=8, replica_groups=mesh['section'=2,'req'=16,'head'=8] {'req'}, dimensions={0}, use_global_device_ids=true | all-gather | bytes 1088 | tf_op jit(solution)/shard_map/all_gather | solution.py:16
  639.3 21.4 %all-gather.16 = f32[16,2,8]{2,1,0:T(2,128)S(1)} all-gather(f32[1,2,8]{2,1,0:T(2,128)S(1)} %bitcast.374), channel_id=9, replica_groups=mesh['section'=2,'req'=16,'head'=8] {'req'}, dimensions={0}, use_global_device_ids=true | all-gather | bytes 1088 | tf_op jit(solution)/shard_map/all_gather | solution.py:16
  660.8 24.0 %all-gather.8 = f32[32,8,128]{2,1,0:T(8,128)S(1)} all-gather(f32[2,8,128]{2,1,0:T(8,128)S(1)} %fusion.32), channel_id=10, replica_groups=mesh['section'=2,'req'=16,'head'=8] {'req'}, dimensions={0}, use_global_device_ids=true | all-gather | bytes 139264 | tf_op jit(solution)/shard_map/all_gather | solution.py:16
  684.7 1.7 while.102
  687.1 1.6 fusion.26
  688.7 13.1 %all_to_all.32 = bf16[16,16,1024]{2,1,0:T(8,128)(2,1)S(1)} all-to-all(bf16[16,16,1024]{2,1,0:T(8,128)(2,1)S(1)} %stack.34), channel_id=1, replica_groups=mesh['section'=2,'req'=16,'head'=8] {'req'}, dimensions={0} | all-to-all | bytes 1048576 | tf_op jit(solution)/shard_map/all_to_all | solution.py:70
  701.8 1.3 fusion.28
  703.2 73.2 %all-reduce.9.cloned.1.call-done = f32[256,512]{1,0:T(8,128)} async-done(((f32[256,512]{1,0:T(8,128)}), f32[256,512]{1,0:T(8,128)}) %all-reduce.9.cloned.1.call-update) | async-done | bytes 524304 | tf_op jit(solution)/shard_map/psum | solution.py:86
  777.5 23.0 %all-gather.17 = f32[16,1,256]{2,1,0:T(1,128)S(1)} all-gather(f32[1,1,256]{2,1,0:T(1,128)S(1)} %bitcast.377), channel_id=11, replica_groups=mesh['section'=2,'req'=16,'head'=8] {'req'}, dimensions={0}, use_global_device_ids=true | all-gather | bytes 17408 | tf_op jit(solution)/shard_map/all_gather | solution.py:16
  801.3 5.0 fusion.54
  806.4 77.7 %reduce-scatter.11.cloned.1.call-done = f32[16,3584]{1,0:T(8,128)} async-done(((f32[256,3584]{1,0:T(8,128)}), f32[16,3584]{1,0:T(8,128)}) %reduce-scatter.11.cloned.1.call-update) | async-done | bytes 229392 | tf_op jit(solution)/shard_map/reduce_scatter | solution.py:77
  885.2 17.5 %all_to_all.33 = bf16[16,16,1792]{2,1,0:T(8,128)(2,1)S(1)} all-to-all(bf16[16,16,1792]{2,1,0:T(8,128)(2,1)S(1)} %stack.35), channel_id=1, replica_groups=mesh['section'=2,'req'=16,'head'=8] {'req'}, dimensions={0} | all-to-all | bytes 1835008 | tf_op jit(solution)/shard_map/all_to_all | solution.py:70
  902.7 1.4 fusion.12
  904.2 73.2 %all-reduce.11.cloned.1.call-done = f32[256,512]{1,0:T(8,128)} async-done(((f32[256,512]{1,0:T(8,128)}), f32[256,512]{1,0:T(8,128)}) %all-reduce.11.cloned.1.call-update) | async-done | bytes 524304 | tf_op jit(solution)/shard_map/psum | solution.py:86
  977.4 1.9 fusion.53
  (363 shorter events, 25.1 us)
Async XLA Ops:
  6.5 411.9 %copy-start = (bf16[1,1792,512]{2,1,0:T(8,128)(2,1)S(1)}, bf16[1,1792,512]{2,1,0:T(8,128)(2,1)}, u32[]{:S(2)}) copy-start(bf16[1,1792,512]{2,1,0:T(8,128)(2,1)} %param.29) | copy-start | bytes 5505028
  6.5 108.0 %reduce-scatter.5.cloned.1.call-start = ((), (), s32[]{:S(2)}) async-start(), calls=%async_computation.10 | async-start | bytes 1392640 | tf_op jit(solution)/shard_map/reduce_scatter | solution.py:77
  32.5 3.1 copy-start.8
  32.5 3.6 copy-start.9
  117.9 11.9 %all-to-all-start = ((bf16[16,2,512]{2,1,0:T(2,128)(2,1)}), bf16[16,2,512]{2,1,0:T(2,128)(2,1)S(1)}, u32[]{:S(2)}, u32[]{:S(2)}) async-start(bf16[16,2,512]{2,1,0:T(2,128)(2,1)} %reshape.847), calls=%async_computation.1 | async-start | bytes 65536 | tf_op jit(solution)/shard_map/all_to_all | solution.py:70
  123.6 168.3 %all-reduce.5.cloned.1.call-start = ((), (), s32[]{:S(2)}) async-start(), calls=%async_computation.11 | async-start | bytes 1048576 | tf_op jit(solution)/shard_map/psum | solution.py:86
  202.6 14.8 %copy-start.3 = (bf16[1,1,1024,512]{3,2,1,0:T(8,128)(2,1)S(1)}, bf16[1,1,1024,512]{3,2,1,0:T(8,128)(2,1)}, u32[]{:S(2)}) copy-start(bf16[1,1,1024,512]{3,2,1,0:T(8,128)(2,1)} %param.26) | copy-start | bytes 3145732
  218.6 181.2 %reduce-scatter.7.cloned.1.call-start = ((), (), s32[]{:S(2)}) async-start(), calls=%async_computation.12 | async-start | bytes 3899392 | tf_op jit(solution)/shard_map/reduce_scatter | solution.py:77
  218.7 4.5 copy-start.7
  218.7 73.2 %copy-start.2 = (bf16[256,512]{1,0:T(8,128)(2,1)S(1)}, bf16[256,512]{1,0:T(8,128)(2,1)}, u32[]{:S(2)}) copy-start(bf16[256,512]{1,0:T(8,128)(2,1)} %param.23) | copy-start | bytes 786436
  293.1 28.8 %copy-start.5 = (bf16[256,512]{1,0:T(8,128)(2,1)}, bf16[256,512]{1,0:T(8,128)(2,1)S(1)}, u32[]{:S(2)}) copy-start(bf16[256,512]{1,0:T(8,128)(2,1)S(1)} %get-tuple-element.863) | copy-start | bytes 786436
  321.9 171.1 %all-reduce.7.cloned.1.call-start = ((), (), s32[]{:S(2)}) async-start(), calls=%async_computation.13 | async-start | bytes 1048576 | tf_op jit(solution)/shard_map/psum | solution.py:86
  419.8 102.4 %copy-start.1 = (bf16[1,512,1,1280]{3,1,2,0:T(8,128)(2,1)S(1)}, bf16[1,512,1,1280]{3,1,2,0:T(8,128)(2,1)}, u32[]{:S(2)}) copy-start(bf16[1,512,1,1280]{3,1,2,0:T(8,128)(2,1)} %param.25) | copy-start | bytes 3932164
  419.8 179.7 %reduce-scatter.9.cloned.1.call-start = ((), (), s32[]{:S(2)}) async-start(), calls=%async_computation.14 | async-start | bytes 1392640 | tf_op jit(solution)/shard_map/reduce_scatter | solution.py:77
  494.9 2.8 collective-permute-start
  602.2 11.9 %all-to-all-start.3 = ((bf16[16,2,512]{2,1,0:T(2,128)(2,1)}), bf16[16,2,512]{2,1,0:T(2,128)(2,1)S(1)}, u32[]{:S(2)}, u32[]{:S(2)}) async-start(bf16[16,2,512]{2,1,0:T(2,128)(2,1)} %reshape.849), calls=%async_computation.6 | async-start | bytes 65536 | tf_op jit(solution)/shard_map/all_to_all | solution.py:70
  607.9 168.5 %all-reduce.9.cloned.1.call-start = ((), (), s32[]{:S(2)}) async-start(), calls=%async_computation.15 | async-start | bytes 1048576 | tf_op jit(solution)/shard_map/psum | solution.py:86
  687.1 14.8 %copy-start.4 = (bf16[1,1,1024,512]{3,2,1,0:T(8,128)(2,1)S(1)}, bf16[1,1,1024,512]{3,2,1,0:T(8,128)(2,1)}, u32[]{:S(2)}) copy-start(bf16[1,1,1024,512]{3,2,1,0:T(8,128)(2,1)} %param.26) | copy-start | bytes 3145732
  688.7 87.7 %copy-start.6 = (bf16[256,512]{1,0:T(8,128)(2,1)S(1)}, bf16[256,512]{1,0:T(8,128)(2,1)}, u32[]{:S(2)}) copy-start(bf16[256,512]{1,0:T(8,128)(2,1)} %get-tuple-element.861) | copy-start | bytes 786436
  703.1 181.0 %reduce-scatter.11.cloned.1.call-start = ((), (), s32[]{:S(2)}) async-start(), calls=%async_computation.16 | async-start | bytes 3899392 | tf_op jit(solution)/shard_map/reduce_scatter | solution.py:77
  806.3 171.0 %all-reduce.11.cloned.1.call-start = ((), (), s32[]{:S(2)}) async-start(), calls=%async_computation.17 | async-start | bytes 1048576 | tf_op jit(solution)/shard_map/psum | solution.py:86
Sparse Core Ops, SparseCore 0:
  35.7 78.7 reduce-scatter.4
  218.7 73.0 all-reduce.4
  322.0 77.7 reduce-scatter.6
  420.0 73.0 all-reduce.6
  524.9 74.5 reduce-scatter.8
  703.2 73.0 all-reduce.8
  806.5 77.6 reduce-scatter.10
  904.3 73.0 all-reduce.10
